TPU v7x, 32 devices: a whole 2x2x4 slice. The times are simulated.
32 devices in a mesh: seq: 4 (over x, core), dp: 8 (over z, y).
Axes of the slice: x: 2, y: 2, z: 4, core: 2. Of those that a mesh axis runs over, the one named last changes fastest.
Arguments:
- tokens: bfloat16 [8, 2048, 2048], P('dp', 'seq'), may hold values from -6 to 6
- log_decay: float32 [8, 8, 2048], P('dp', None, 'seq'), may hold values from -1 to 0
- w_qkv: bfloat16 [2048, 3072], P('dp'), may hold values from -0.125 to 0.125
- w_gate: bfloat16 [2048, 1024], P('dp'), may hold values from -0.125 to 0.125
- w_out: bfloat16 [1024, 2048], P('dp'), may hold values from -0.1875 to 0.1875
- norm_gain: float32 [1024], replicated, may hold values from 0.1 to 1.9
Outputs:
- mixed_rows: bfloat16 [8, 2048, 2048], P('dp', 'seq')
All inputs are finite; a program needn't handle non-finite values.
Results may differ from a plain program's by a relative error of at most 0.0065.
Values may be sent and summed in bfloat16 or wider, within the bound.
A program may use at most 64 MiB of HBM per device.

v0:
```python
import jax
import jax.numpy as jnp
from jax import lax
from jax.sharding import PartitionSpec as P


def fold_states(carried, piece, before, block_totals, my_index):
    span = piece.shape[0]
    mine = lax.dynamic_index_in_dim(before, my_index, 0, keepdims=False)
    order = jnp.arange(span, dtype=jnp.int32)
    earlier = (order < my_index)[:, None]
    decay_gap = mine[None, :] - before - block_totals
    factor = jnp.where(earlier, jnp.exp(jnp.where(earlier, decay_gap, 0.0)), 0.0)
    return carried + jnp.einsum("jh,jhde->hde", factor, piece, precision=lax.Precision.HIGHEST)


def body(tokens, log_decay, w_qkv, w_gate, w_out, norm_gain):
    tok_rows = tokens[0]
    tok_count = tok_rows.shape[0]
    head_count = log_decay.shape[1]
    feat_count = norm_gain.shape[0]
    head_dim = feat_count // head_count
    seq_count = lax.axis_size("seq")
    seq_index = lax.axis_index("seq")
    qkv_width = w_qkv.shape[1] // seq_count
    gate_width = w_gate.shape[1] // seq_count
    slab_width = qkv_width + gate_width
    qkv_slab = lax.dynamic_slice_in_dim(w_qkv, seq_index * qkv_width, qkv_width, 1)
    gate_slab = lax.dynamic_slice_in_dim(w_gate, seq_index * gate_width, gate_width, 1)
    column_slab = jnp.concatenate([qkv_slab, gate_slab], axis=1)
    full_rows = lax.all_gather(column_slab, "dp", axis=0, tiled=True)
    piece = lax.all_gather(full_rows, "seq", axis=1, tiled=True)
    slab_count = piece.shape[1] // slab_width
    product = jnp.dot(tok_rows, piece, preferred_element_type=jnp.float32).reshape(
        tok_count, slab_count, slab_width
    )
    qkv_total = product[:, :, :qkv_width]
    gate_total = product[:, :, qkv_width:]
    projected = qkv_total.reshape(tok_count, seq_count * qkv_width)
    gate_pre = gate_total.reshape(tok_count, seq_count * gate_width)
    activated = (
        jax.nn.silu(projected).astype(jnp.bfloat16).reshape(tok_count, 3, head_count, head_dim)
    )
    query_rows = activated[:, 0]
    key_rows = activated[:, 1]
    value_rows = activated[:, 2]
    cum_decay = jnp.cumsum(log_decay[0], axis=1)
    block_decay = cum_decay[:, -1]
    key_factor = jnp.exp(block_decay[:, None] - cum_decay).T
    scaled_key = (key_rows.astype(jnp.float32) * key_factor[:, :, None]).astype(jnp.bfloat16)
    local_state = jnp.einsum(
        "thd,the->hde", scaled_key, value_rows, preferred_element_type=jnp.float32
    )
    my_index = lax.axis_index("seq")
    empty_state = jnp.zeros((head_count, head_dim, head_dim), jnp.float32)
    all_states, all_decays = (
        lax.all_gather(local_state[None].astype(jnp.bfloat16), "seq", axis=0, tiled=True).astype(
            jnp.float32
        ),
        lax.all_gather(block_decay[None].astype(jnp.bfloat16), "seq", axis=0, tiled=True).astype(
            jnp.float32
        ),
    )
    before = jnp.cumsum(all_decays, axis=0) - all_decays
    carried = fold_states(empty_state, all_states, before, all_decays, my_index)
    scores = jnp.einsum("thd,shd->hts", query_rows, key_rows, preferred_element_type=jnp.float32)
    positions = jnp.arange(tok_count, dtype=jnp.int32)
    causal_mask = (positions[None, :] <= positions[:, None])[None, :, :]
    decay_gap = cum_decay[:, :, None] - cum_decay[:, None, :]
    decay_mat = jnp.where(causal_mask, jnp.exp(jnp.where(causal_mask, decay_gap, 0.0)), 0.0)
    weighted = (scores * decay_mat).astype(jnp.bfloat16)
    intra_part = jnp.einsum(
        "hts,shd->thd", weighted, value_rows, preferred_element_type=jnp.float32
    )
    query_scaled = query_rows.astype(jnp.float32) * jnp.exp(cum_decay).T[:, :, None]
    inter_part = jnp.einsum("thd,hde->the", query_scaled, carried, precision=lax.Precision.HIGHEST)
    attended = (intra_part + inter_part).reshape(tok_count, feat_count)
    mean_square = jnp.mean(attended * attended, axis=1, keepdims=True)
    normed = attended * lax.rsqrt(mean_square + 1e-06) * norm_gain
    gated = (normed * jax.nn.sigmoid(gate_pre)).astype(jnp.bfloat16)
    out_sum = jnp.dot(
        gated, lax.all_gather(w_out, "dp", axis=0, tiled=True), preferred_element_type=jnp.float32
    )
    return out_sum.astype(jnp.bfloat16)[None]


def solution(mesh):
    placed = (
        P("dp", "seq", None),
        P("dp", None, "seq"),
        P("dp", None),
        P("dp", None),
        P("dp", None),
        P(),
    )
    return jax.shard_map(
        body, mesh=mesh, in_specs=placed, out_specs=P("dp", "seq", None), check_vma=False
    )
```

profile of v0, /device:TPU:0, one launch (start us, length us, event | category | flops | bytes accessed | tf_op | source)
XLA Modules:
  0.0 327.2 jit_solution(16576440834460175521)
XLA Ops:
  6.5 0.0 copy-start
  6.5 0.0 all-gather.7.cloned.1.call-start
  6.5 1.2 constant_dynamic-slice_fusion.2
  7.7 0.0 copy-start.4
  7.7 0.9 constant_dynamic-slice_fusion.1
  8.7 0.9 pad_maximum_fusion
  9.5 0.0 all-gather.7.cloned.1.call-update
  9.5 0.0 all-gather.9.cloned.1.call-start
  9.6 75.6 %all-gather.7.cloned.1.call-done = bf16[2048,1024]{1,0:T(8,128)(2,1)} async-done(((bf16[256,1024]{1,0:T(8,128)(2,1)}), bf16[2048,1024]{1,0:T(8,128)(2,1)}) %all-gather.7.cloned.1.call-update) | async-done | bytes 4194320 | tf_op jit(solution)/shard_map/all_gather | solution.py:31
  85.2 0.0 all-gather.9.cloned.1.call-update
  85.2 0.0 all-gather.13.cloned.1.call-start
  85.3 0.0 copy-done.4
  85.3 1.1 reduce-window.6
  86.4 0.2 slice_reduce_fusion
  86.6 0.1 exponential_bitcast_fusion
  86.7 0.2 slice_reduce_fusion.1
  86.9 0.1 exponential_bitcast_fusion.1
  87.0 104.2 %all-gather.9.cloned.1.call-done = bf16[2048,4096]{1,0:T(8,128)(2,1)} async-done(((bf16[2048,1024]{1,0:T(8,128)(2,1)}), bf16[2048,4096]{1,0:T(8,128)(2,1)}) %all-gather.9.cloned.1.call-update) | async-done | bytes 16777232 | tf_op jit(solution)/shard_map/all_gather | solution.py:32
  191.2 0.0 copy-done
  191.2 11.7 %fusion.12 = f32[4096,512]{1,0:T(8,128)S(1)} fusion(bf16[2048,4096]{1,0:T(8,128)(2,1)} %all-gather.9.cloned.1.call-done, bf16[1,512,2048]{2,1,0:T(8,128)(2,1)S(1)} %copy-done), kind=kOutput, calls=%fused_computation.17 | convolution fusion | flops 8589934592 | bytes 27262976 | tf_op jit(solution)/shard_map/dot_general | solution.py:34
  203.0 0.0 copy-start.1
  203.0 3.8 %slice.32 = f32[512,4,768]{0,2,1:T(8,128)} slice(f32[512,4,1024]{0,2,1:T(8,128)S(1)} %bitcast.65), slice={[0:512], [0:4], [0:768]} | slice | bytes 12582912 | tf_op jit(solution)/shard_map/slice | solution.py:37
  206.8 1.3 copy-done.1
  208.1 6.6 %copy.22 = f32[512,3,8,128]{3,0,2,1:T(8,128)} copy(f32[512,3,8,128]{0,3,2,1:T(8,128)} %bitcast.64) | data formatting | bytes 12582912 | tf_op jit(solution)/shard_map/reshape | solution.py:39
  214.7 4.4 %multiply_convert_fusion.1 = bf16[512,3,8,128]{3,0,2,1:T(8,128)(2,1)S(1)} fusion(f32[512,3,8,128]{3,0,2,1:T(8,128)} %copy.22), kind=kLoop, calls=%fused_computation.1 | loop fusion | flops 7864320 | bytes 9437184 | tf_op jit(solution)/shard_map/convert_element_type | solution.py:42
  219.1 0.0 copy-start.3
  219.1 1.7 copy-done.3
  220.8 0.0 copy-start.6
  220.8 2.3 convolution_convert_fusion.1
  223.1 0.0 all-gather.13.cloned.1.call-update
  223.1 0.0 all-gather.11.cloned.1.call-start
  223.2 0.5 all-gather.11.cloned.1.call-update
  223.7 0.0 copy-done.6
  223.7 0.6 dynamic-slice
  224.9 0.2 fusion.22
  225.1 0.2 dynamic-update-slice
  225.4 6.1 %all-reduce = bf16[32]{0:T(256)(128)(2,1)S(1)} all-reduce(bf16[32]{0:T(256)(128)(2,1)S(1)} %dynamic-update-slice), channel_id=2, replica_groups=mesh['seq'=4,'dp'=8] {'seq'}, use_global_device_ids=true, to_apply=%add | all-reduce | flops 32 | bytes 128
  231.4 0.1 reshape.101
  231.6 0.1 iota_compare_fusion
  231.7 0.1 select_bitcast_fusion
  231.8 3.5 %fusion.7 = f32[512,4,256]{0,2,1:T(8,128)} fusion(f32[512,4,1024]{0,2,1:T(8,128)} %bitcast.66), kind=kLoop, calls=%fused_computation.10 | loop fusion | flops 1572864 | bytes 4194304 | tf_op jit(solution)/shard_map/div | solution.py:80
  235.2 6.7 %fusion = f32[8,128,512]{2,1,0:T(8,128)} fusion(f32[8,512]{1,0:T(8,128)S(1)} %get-tuple-element.6, pred[512,512]{1,0:T(8,128)(4,1)S(1)} %iota_compare_fusion, bf16[512,3,8,128]{3,0,2,1:T(8,128)(2,1)} %copy-done.3), kind=kOutput, calls=%fused_computation.2 | convolution fusion | flops 1084227584 | bytes 5537792 | tf_op jit(solution)/shard_map/hts,shd->thd/dot_general | solution.py:72
  242.0 0.0 all-gather.13.cloned.1.call-done
  242.0 1.6 multiply_reduce_fusion
  243.5 0.0 copy-start.2
  243.5 0.0 copy-start.5
  243.6 4.8 %fusion.11 = (f32[512]{0:T(512)S(1)}, f32[8,128,512]{2,1,0:T(8,128)S(1)}) fusion(f32[8,128,512]{2,1,0:T(8,128)} %fusion, f32[8,128,128]{2,1,0:T(8,128)S(1)} %multiply_reduce_fusion, f32[512,8]{0,1:T(8,128)S(1)} %get-tuple-element.5, bf16[512,3,8,128]{3,0,2,1:T(8,128)(2,1)} %copy-done.3), kind=kOutput, calls=%fused_computation.16 | convolution fusion | flops 807927296 | bytes 5785600 | tf_op jit(solution)/shard_map/thd,hde->the/dot_general | solution.py:76
  248.4 0.0 copy-done.2
  248.4 0.0 copy-done.5
  248.4 0.3 fusion.10
  248.7 66.0 %all-gather.11.cloned.1.call-done = bf16[1024,2048]{1,0:T(8,128)(2,1)} async-done(((bf16[128,2048]{1,0:T(8,128)(2,1)}), bf16[1024,2048]{1,0:T(8,128)(2,1)}) %all-gather.11.cloned.1.call-update) | async-done | bytes 4194320 | tf_op jit(solution)/shard_map/all_gather | solution.py:82
  314.8 5.9 %fusion.4 = bf16[1,512,2048]{2,1,0:T(8,128)(2,1)} fusion(bf16[512,1024]{0,1:T(8,128)(2,1)S(1)} %fusion.10, bf16[1024,2048]{1,0:T(8,128)(2,1)} %all-gather.11.cloned.1.call-done), kind=kOutput, calls=%fused_computation.6 | convolution fusion | flops 2148532224 | bytes 7340032 | tf_op jit(solution)/shard_map/dot_general | solution.py:81
  (8 shorter events, 0.1 us)
Async XLA Ops:
  6.5 184.7 %copy-start = (bf16[1,512,2048]{2,1,0:T(8,128)(2,1)S(1)}, bf16[1,512,2048]{2,1,0:T(8,128)(2,1)}, u32[]{:S(2)}) copy-start(bf16[1,512,2048]{2,1,0:T(8,128)(2,1)} %param.6) | copy-start | bytes 6291460
  6.5 78.7 %all-gather.7.cloned.1.call-start = ((), (), s32[]{:S(2)}) async-start(), calls=%async_computation | async-start | bytes 4718592 | tf_op jit(solution)/shard_map/all_gather | solution.py:31
  7.7 77.6 %copy-start.4 = (f32[1,8,512]{2,1,0:T(8,128)S(1)}, f32[1,8,512]{2,1,0:T(8,128)}, u32[]{:S(2)}) copy-start(f32[1,8,512]{2,1,0:T(8,128)} %param.7) | copy-start | bytes 49156
  9.5 181.7 %all-gather.9.cloned.1.call-start = ((), (), s32[]{:S(2)}) async-start(), calls=%async_computation.1 | async-start | bytes 20971520 | tf_op jit(solution)/shard_map/all_gather | solution.py:32
  85.2 156.7 %all-gather.13.cloned.1.call-start = ((), (), s32[]{:S(2)}) async-start(), calls=%async_computation.3 | async-start | bytes 1310720 | tf_op jit(solution)/shard_map/all_gather | solution.py:57
  203.0 5.1 %copy-start.1 = (f32[4096,512]{1,0:T(8,128)}, f32[4096,512]{1,0:T(8,128)S(1)}, u32[]{:S(2)}) copy-start(f32[4096,512]{1,0:T(8,128)S(1)} %fusion.12) | copy-start | bytes 25165828
  219.1 1.7 copy-start.3
  220.8 2.9 copy-start.6
  223.1 91.7 %all-gather.11.cloned.1.call-start = ((), (), s32[]{:S(2)}) async-start(), calls=%async_computation.2 | async-start | bytes 4718592 | tf_op jit(solution)/shard_map/all_gather | solution.py:82
  243.5 4.9 %copy-start.2 = (f32[512,4,256]{0,2,1:T(8,128)S(1)}, f32[512,4,256]{0,2,1:T(8,128)}, u32[]{:S(2)}) copy-start(f32[512,4,256]{0,2,1:T(8,128)} %fusion.7) | copy-start | bytes 6291460
  243.5 4.9 %copy-start.5 = (f32[1024]{0:T(1024)S(1)}, f32[1024]{0:T(1024)}, u32[]{:S(2)}) copy-start(f32[1024]{0:T(1024)} %param.11) | copy-start | bytes 12292
Sparse Core Ops, SparseCore 0:
  9.7 75.5 all-gather.6
  86.8 104.4 all-gather.8
  223.2 16.6 all-gather.12
  241.9 72.7 all-gather.10
where the time goes:
time: 328 us; the launch traced here: 327 us
  waiting for transfers between devices  246 us (75%)
  matrix products  31.5 us (10%)
  local copies, waits for them, and re-layouts  16.9 us (5%)
  between operations  13.9 us (4%)
  other arithmetic  12.2 us (4%)
  blocking collectives  6.06 us (2%)
    all_gather x1, waiting for transfers between devices, body(): piece = lax.all_gather(full_rows, 'seq', axis=1, tiled=True)  104 us
    all_gather x1, waiting for transfers between devices, body(): full_rows = lax.all_gather(column_slab, 'dp', axis=0, tiled=True)  75.6 us
    all_gather x1, waiting for transfers between devices, body(): lax.all_gather(w_out, 'dp', axis=0, tiled=True)  66 us
    dot_general x1, matrix products, body(): jnp.dot(tok_rows, piece, preferred_element_type=jnp.float32)  11.7 us
    dot_general x1, matrix products, body(): jnp.einsum('hts,shd->thd', weighted, value_rows, preferred_element_type=j...  6.75 us
    reshape x1, local copies, waits for them, and re-layouts, body(): projected = qkv_total.reshape(tok_count, seq_count * qkv_width)  6.59 us
  transfers between devices with their start and end apart: 4, of which 3 were waited for; matrix products, arithmetic and copies ran while one was open for 6% of the time, Pallas kernels for 0%

commit v1 on v0

v1 whole, which is shorter than its diff:
```python
import functools

import jax
import jax.numpy as jnp
from jax import lax
from jax.experimental import pallas as pl
from jax.experimental.pallas import tpu as pltpu
from jax.sharding import PartitionSpec as P

MESH = pl.DeviceIdType.MESH
F32 = jnp.float32
BF16 = jnp.bfloat16


def fused(n_dp, n_seq, tok, ld, gain, wqkv, wgate, wout, out, W, WO, acc, lhs, q_s, k_s, v_s,
          att, ccol, crow, ss, gated, st_local, st_recv, st_send, loc_sem,
          rr, pr, xr, pxr, rs, ps, xs, pxs, ch_s, ch_r):
    T, D = tok.shape
    H = ld.shape[0]
    F = gain.shape[1]
    hd = F // H
    N = n_dp
    s = lax.axis_index("seq")
    d = lax.axis_index("dp")
    core = s % 2
    x = (s // 2) % 2
    partner = s + 1 - 2 * core
    xpeer = s + 2 - 4 * x
    half = N // 2

    def pos_of(i):
        return jnp.where(i % 2 == 0, i // 2, N - 1 - i // 2)

    def dev_at(p):
        p = lax.rem(p + 2 * N, N)
        return jnp.where(p < half, 2 * p, 2 * (N - 1 - p) + 1)

    pos = pos_of(d)
    ring_to = (dev_at(pos + 1), dev_at(pos - 1))

    def origin(dr, k):
        return dev_at(pos - k) if dr == 0 else dev_at(pos + k)

    E = (F + F // 4, 5 * D // 16)
    M = (F + F // 2, D - 2 * (5 * D // 16))
    bufs = (W, WO)
    rows_of = (D // N, F // N)

    def piece(ph, dr, k, c, excl, xb):
        R = rows_of[ph]
        q = R // 4
        row = pl.multiple_of(origin(dr, k) * R + dr * (R // 2) + c * q, q)
        if excl:
            col = pl.multiple_of(xb * (E[ph] + M[ph]), 128)
            return bufs[ph].at[pl.ds(row, q), pl.ds(col, E[ph])]
        return bufs[ph].at[pl.ds(row, q), pl.ds(E[ph], M[ph])]

    def mk(ref, ssem, rsem, dev):
        return pltpu.make_async_remote_copy(
            src_ref=ref, dst_ref=ref, send_sem=ssem, recv_sem=rsem,
            device_id=dev, device_id_type=MESH)

    def dev(seq=None, dp=None):
        return {"seq": s if seq is None else seq, "dp": d if dp is None else dp}

    def ring_desc(ph, dr, k, at, p):
        return mk(piece(ph, dr, at, core, p == 0, x), rs.at[ph, dr, p, k % 2],
                  rr.at[ph, dr, k - 1, p], dev(dp=ring_to[dr]))

    def part_desc(ph, dr, k, c, p):
        return mk(piece(ph, dr, k, c, p == 0, x), ps.at[ph, dr, p, k % 2],
                  pr.at[ph, dr, k - 1, p], dev(seq=partner))

    def x_desc(ph, dr, k, xb):
        return mk(piece(ph, dr, k, core, True, xb), xs.at[ph, dr, k % 2],
                  xr.at[ph, dr, k - 1], dev(seq=xpeer))

    def px_desc(ph, dr, k, c):
        return mk(piece(ph, dr, k, c, True, 1 - x), pxs.at[ph, dr, k % 2],
                  pxr.at[ph, dr, k - 1], dev(seq=partner))

    def send(desc, k):
        @pl.when(k > 2)
        def _():
            desc.wait_send()
        desc.start()

    def relay(ph, k):
        for p in (0, 1):
            for dr in (0, 1):
                ring_desc(ph, dr, k, k, p).wait_recv()

                @pl.when(k < N - 1)
                def _():
                    send(ring_desc(ph, dr, k + 1, k, p), k + 1)
                if p == 0:
                    send(x_desc(ph, dr, k, x), k)
                send(part_desc(ph, dr, k, core, p), k)

    def xrelay(ph, k):
        for dr in (0, 1):
            x_desc(ph, dr, k, 1 - x).wait_recv()
            send(px_desc(ph, dr, k, core), k)

    def collect(ph, k):
        for dr in (0, 1):
            for p in (0, 1):
                part_desc(ph, dr, k, 1 - core, p).wait_recv()
            px_desc(ph, dr, k, 1 - core).wait_recv()

    def drain(ph):
        for k in (N - 2, N - 1):
            for dr in (0, 1):
                for p in (0, 1):
                    ring_desc(ph, dr, k, k, p).wait_send()
                    part_desc(ph, dr, k, core, p).wait_send()
                x_desc(ph, dr, k, x).wait_send()
                px_desc(ph, dr, k, core).wait_send()

    R = D // N
    RO = F // N
    g = F // 4
    base = pl.multiple_of(d * R, R)
    src_dst = (
        (wqkv.at[:, pl.ds(0, F)], 0, F), (wgate.at[:, pl.ds(0, g)], F, g),
        (wqkv.at[:, pl.ds(F, F)], F + g, F), (wgate.at[:, pl.ds(g, 2 * g)], 2 * F + g, 2 * g),
        (wqkv.at[:, pl.ds(2 * F, F)], 2 * F + 3 * g, F),
        (wgate.at[:, pl.ds(3 * g, g)], 3 * F + 3 * g, g),
    )
    loads = [pltpu.make_async_copy(a, W.at[pl.ds(base, R), pl.ds(c0, w)], loc_sem.at[i])
             for i, (a, c0, w) in enumerate(src_dst)]
    loads.append(pltpu.make_async_copy(
        wout, WO.at[pl.ds(pl.multiple_of(d * RO, RO), RO), :], loc_sem.at[6]))
    for c in loads:
        c.start()

    barrier = pltpu.get_barrier_semaphore()
    for who in (dev(dp=ring_to[0]), dev(dp=ring_to[1]), dev(seq=partner), dev(seq=xpeer)):
        pl.semaphore_signal(barrier, inc=1, device_id=who, device_id_type=MESH)

    @pl.when(s > 0)
    def _():
        pl.semaphore_signal(barrier, inc=1, device_id=dev(seq=s - 1), device_id_type=MESH)

    @pl.when(s < n_seq - 1)
    def _():
        pl.semaphore_signal(barrier, inc=1, device_id=dev(seq=s + 1), device_id_type=MESH)
    for c in loads:
        c.wait()
    pl.semaphore_wait(barrier, 4 + jnp.where(s > 0, 1, 0) + jnp.where(s < n_seq - 1, 1, 0))

    for p in (0, 1):
        for dr in (0, 1):
            ring_desc(0, dr, 1, 0, p).start()

    cum = ld[...]
    lane = lax.broadcasted_iota(jnp.int32, (H, T), 1)
    step = 1
    while step < T:
        cum = cum + jnp.where(lane >= step, pltpu.roll(cum, step, 1), 0.0)
        step *= 2
    for h in range(H):
        crow[h] = jnp.broadcast_to(cum[h:h + 1, :], (8, T))
        ccol[h] = jnp.broadcast_to(cum[h:h + 1, :], (hd, T)).T

    tile = F // 2
    tiles = 4 * F // tile
    hr = R // 2

    def chunk(k):
        o = [origin(dr, k) for dr in (0, 1)]
        rows = []
        for dr in (0, 1):
            b = pl.multiple_of(o[dr] * R, R)
            lhs[:, dr * hr:(dr + 1) * hr] = tok[:, pl.ds(b, R)][:, dr * hr:(dr + 1) * hr]
            rows.append(pl.ds(pl.multiple_of(b + dr * hr, hr), hr))

        @pl.loop(0, tiles)
        def _(j):
            cols = pl.ds(pl.multiple_of(j * tile, tile), tile)
            w = jnp.concatenate([W[rows[0], cols], W[rows[1], cols]], axis=0)
            acc[:, cols] += jnp.dot(lhs[...], w, preferred_element_type=F32)

    @pl.loop(0, tiles)
    def _(j):
        cols = pl.ds(pl.multiple_of(j * tile, tile), tile)
        acc[:, cols] = jnp.dot(tok[:, pl.ds(base, R)], W[pl.ds(base, R), cols],
                               preferred_element_type=F32)

    def op(k):
        @pl.when(k <= N - 1)
        def _():
            relay(1, k)

        @pl.when(jnp.logical_and(k >= 2, k <= N))
        def _():
            xrelay(1, k - 1)

    @pl.loop(1, N + 2)
    def _(t):
        @pl.when(t <= N - 1)
        def _():
            relay(0, t)

        @pl.when(t == N - 2)
        def _():
            for p in (0, 1):
                for dr in (0, 1):
                    ring_desc(1, dr, 1, 0, p).start()

        @pl.when(jnp.logical_and(t >= 2, t <= N))
        def _():
            xrelay(0, t - 1)

        @pl.when(t >= N)
        def _():
            op(t - N + 1)

        @pl.when(t >= 3)
        def _():
            collect(0, t - 2)
            chunk(t - 2)

    def silu(v):
        return (v / (1.0 + jnp.exp(-v))).astype(BF16)

    def cols_at(c):
        return pl.ds(pl.multiple_of(c, 128), hd)

    @pl.loop(0, H)
    def _(h):
        kk = silu(acc[:, cols_at(F + g + h * hd)])
        vv = silu(acc[:, cols_at(2 * F + 3 * g + h * hd)])
        k_s[h] = kk
        v_s[h] = vv
        q_s[h] = silu(acc[:, cols_at(h * hd)])
        c = ccol[h]
        sk = (kk.astype(F32) * jnp.exp(c[T - 1:T, :] - c)).astype(BF16)
        st_local[h] = lax.dot_general(sk, vv, (((0,), (0,)), ((), ())),
                                      preferred_element_type=F32)

    def chain_desc(to):
        return pltpu.make_async_remote_copy(
            src_ref=st_send, dst_ref=st_recv, send_sem=ch_s, recv_sem=ch_r,
            device_id=dev(seq=to), device_id_type=MESH)

    @pl.when(s == 0)
    def _():
        st_recv[...] = jnp.zeros_like(st_recv)
        st_send[...] = st_local[...].astype(BF16)
        chain_desc(s + 1).start()

    blk = T // 2
    tri = (lax.broadcasted_iota(jnp.int32, (blk, blk), 1)
           <= lax.broadcasted_iota(jnp.int32, (blk, blk), 0))

    @pl.loop(0, H)
    def _(h):
        op(h + 3)
        for b in (0, 1):
            r = slice(b * blk, (b + 1) * blk)
            q = q_s[h, r, :]
            c = jnp.concatenate([ccol[h, r, :]] * (blk // hd), axis=1)
            total = None
            for e in range(b + 1):
                z = slice(e * blk, (e + 1) * blk)
                sc = lax.dot_general(q, k_s[h, z, :], (((1,), (1,)), ((), ())),
                                     preferred_element_type=F32)
                gap = c - crow[h, 0:1, z]
                if e == b:
                    gap = jnp.where(tri, gap, -1e30)
                w = (sc * jnp.exp(gap)).astype(BF16)
                y = jnp.dot(w, v_s[h, z, :], preferred_element_type=F32)
                total = y if total is None else total + y
            att[h, r, :] = total

        @pl.when(jnp.logical_and(s > 0, h == (s * H) // n_seq))
        def _():
            chain_desc(s).wait_recv()

            @pl.when(s < n_seq - 1)
            def _():
                for j in range(H):
                    keep = jnp.exp(ccol[j, T - 1:T, :])
                    st_send[j] = (keep * st_recv[j].astype(F32) + st_local[j]).astype(BF16)
                chain_desc(s + 1).start()

    if N > H + 2:
        @pl.loop(H + 3, N + 1)
        def _(k):
            op(k)

    ss[...] = jnp.zeros_like(ss)

    @pl.loop(0, H)
    def _(h):
        inter = jnp.dot(q_s[h], st_recv[h], preferred_element_type=F32)
        a = att[h] + inter * jnp.exp(ccol[h])
        att[h] = a
        ss[...] += a * a

    inv = lax.rsqrt(jnp.sum(ss[...], axis=1, keepdims=True) * (1.0 / F) + 1e-06)
    ss[...] = jnp.broadcast_to(inv, ss.shape)

    @pl.loop(0, H)
    def _(h):
        f = h * hd
        gc = jnp.where(f < g, F + f, jnp.where(f < 3 * g, 2 * F + f, 3 * F + f))
        gate = 1.0 / (1.0 + jnp.exp(-acc[:, cols_at(gc)]))
        gated[:, cols_at(f)] = (att[h] * ss[...] * gain[:, cols_at(f)] * gate).astype(BF16)

    @pl.loop(1, N)
    def _(k):
        collect(1, k)

    @pl.loop(0, D // tile)
    def _(j):
        cols = pl.ds(pl.multiple_of(j * tile, tile), tile)
        out[:, cols] = jnp.dot(gated[...], WO[:, cols], preferred_element_type=F32).astype(BF16)

    drain(0)
    drain(1)

    @pl.when(s < n_seq - 1)
    def _():
        chain_desc(s + 1).wait_send()


def body(n_dp, n_seq, tokens, log_decay, w_qkv, w_gate, w_out, norm_gain):
    tok = tokens[0]
    T, D = tok.shape
    H = log_decay.shape[1]
    F = norm_gain.shape[0]
    hd = F // H
    R = D // n_dp
    vm = pl.BlockSpec(memory_space=pltpu.VMEM)
    hbm = pl.BlockSpec(memory_space=pl.ANY)
    dma = pltpu.SemaphoreType.DMA
    n = n_dp - 1
    y = pl.pallas_call(
        functools.partial(fused, n_dp, n_seq),
        out_shape=jax.ShapeDtypeStruct((T, D), BF16),
        in_specs=[vm, vm, vm, hbm, hbm, hbm],
        out_specs=vm,
        scratch_shapes=[
            pltpu.VMEM((D, 4 * F), BF16), pltpu.VMEM((F, D), BF16),
            pltpu.VMEM((T, 4 * F), F32), pltpu.VMEM((T, R), BF16),
            pltpu.VMEM((H, T, hd), BF16), pltpu.VMEM((H, T, hd), BF16),
            pltpu.VMEM((H, T, hd), BF16), pltpu.VMEM((H, T, hd), F32),
            pltpu.VMEM((H, T, hd), F32), pltpu.VMEM((H, 8, T), F32),
            pltpu.VMEM((T, hd), F32), pltpu.VMEM((T, F), BF16),
            pltpu.VMEM((H, hd, hd), F32), pltpu.VMEM((H, hd, hd), BF16),
            pltpu.VMEM((H, hd, hd), BF16),
            dma((7,)),
            dma((2, 2, n, 2)), dma((2, 2, n, 2)), dma((2, 2, n)), dma((2, 2, n)),
            dma((2, 2, 2, 2)), dma((2, 2, 2, 2)), dma((2, 2, 2)), dma((2, 2, 2)),
            dma, dma,
        ],
        compiler_params=pltpu.CompilerParams(
            collective_id=0, has_side_effects=True, vmem_limit_bytes=60 * 1024 * 1024),
    )(tok, log_decay[0], norm_gain[None], w_qkv, w_gate, w_out)
    return y[None]


def solution(mesh):
    placed = (
        P("dp", "seq", None),
        P("dp", None, "seq"),
        P("dp", None),
        P("dp", None),
        P("dp", None),
        P(),
    )
    return jax.shard_map(
        functools.partial(body, mesh.shape["dp"], mesh.shape["seq"]),
        mesh=mesh, in_specs=placed, out_specs=P("dp", "seq", None), check_vma=False
    )
```

time: 328 us -> 107 us (0.33)
  waiting for transfers between devices: 246 us -> 0 us
  Pallas kernels: 0 us -> 103 us
  matrix products: 31.5 us -> 0 us
  between operations: 13.9 us -> 0.01 us
  local copies, waits for them, and re-layouts: 16.9 us -> 3.16 us
  other arithmetic: 12.2 us -> 0 us
  blocking collectives: 6.06 us -> 0 us
    all_gather x4 -> x0, waiting for transfers between devices: 246 us -> none  [the longest x1 104 us: body(): piece = lax.all_gather(full_rows, 'seq', axis=1, tiled=True)]
    pallas_call x0 -> x1, Pallas kernels: none -> 103 us  [body(): pl.pallas_call(functools.partial(fused, n_dp, n_seq), out_shape=jax.Shape...]
    dot_general x5 -> x0, matrix products: 31.5 us -> none  [the longest x1 11.7 us: body(): jnp.dot(tok_rows, piece, preferred_element_type=jnp.float32)]
    reshape x1 -> x0, local copies, waits for them, and re-layouts: 6.59 us -> none  [body(): projected = qkv_total.reshape(tok_count, seq_count * qkv_width)]
    unnamed x1 -> x0, blocking collectives: 6.06 us -> none
    convert_element_type x2 -> x0, other arithmetic: 4.74 us -> none  [the longest x1 4.43 us: body(): jax.nn.silu(projected).astype(jnp.bfloat16)]
    slice x3 -> x0, local copies, waits for them, and re-layouts: 4.19 us -> none  [the longest x1 3.85 us: body(): qkv_total = product[:, :, :qkv_width]]
    div x1 -> x0, other arithmetic: 3.46 us -> none  [body(): gated = (normed * jax.nn.sigmoid(gate_pre)).astype(jnp.bfloat16)]
  transfers between devices with their start and end apart: 4 -> 0, of which waited for: 3 -> 0; matrix products, arithmetic and copies ran while one was open for 6% -> 0% of each run, Pallas kernels for 0% -> 0%
where the time goes in v1:
time: 107 us; the launch traced here: 106 us
  Pallas kernels  103 us (96%)
  local copies, waits for them, and re-layouts  3.16 us (3%)
    pallas_call x1, Pallas kernels, body(): pl.pallas_call(functools.partial(fused, n_dp, n_seq), out_shape=jax.Shape...  103 us
    unnamed x1, local copies, waits for them, and re-layouts  3.16 us

profile of v1, /device:TPU:0, one launch (start us, length us, event | category | flops | bytes accessed | tf_op | source)
XLA Modules:
  0.0 106.4 jit_solution(11543404345053058339)
XLA Ops:
  0.0 103.2 %shard_map.64 = bf16[512,2048]{1,0:T(8,128)(2,1)} custom-call(bf16[512,2048]{1,0:T(8,128)(2,1)} %bitcast.5, f32[8,512]{1,0:T(8,128)} %bitcast.6, f32[1,1024]{1,0:T(1,128)} %bitcast.7, bf16[256,3072]{1,0:T(8,128)(2,1)} %wqkv.1, bf16[256,1024]{1,0:T(8,128)(2,1)} %wgate.1, bf16[128,2048]{1,0:T(8,128)(2,1)} %wout.1), custom_call_target="tpu_custom_call" | custom-call | tf_op jit(solution)/shard_map/pallas_call | solution.py:340
  103.2 3.2 %copy.8 = bf16[1,512,2048]{2,1,0:T(8,128)(2,1)} copy(bf16[1,512,2048]{2,1,0:T(8,128)(2,1)} %bitcast.4) | data formatting | bytes 4194304

commit v2 on v1

--- a/solution.py
+++ b/solution.py
@@ -12,10 +12,11 @@
 BF16 = jnp.bfloat16
 
 
-def fused(n_dp, n_seq, tok, ld, gain, wqkv, wgate, wout, out, W, WO, acc, lhs, q_s, k_s, v_s,
+def fused(n_dp, n_seq, tok_hbm, ld, gain, wqkv, wgate, wout, out, tok, ob, W, WO, acc, lhs, q_s, k_s, v_s,
           att, ccol, crow, ss, gated, st_local, st_recv, st_send, loc_sem,
-          rr, pr, xr, pxr, rs, ps, xs, pxs, ch_s, ch_r):
-    T, D = tok.shape
+          tok_sem, out_sem, rr, pr, xr, pxr, rs, ps, xs, pxs,
+          rr1, pr1, xr1, pxr1, rs1, ps1, xs1, pxs1, ch_s, ch_r):
+    T, D = tok_hbm.shape
     H = ld.shape[0]
     F = gain.shape[1]
     hd = F // H
@@ -46,10 +47,20 @@
     bufs = (W, WO)
     rows_of = (D // N, F // N)
 
+    sems = ((rr, pr, xr, pxr, rs, ps, xs, pxs), (rr1, pr1, xr1, pxr1, rs1, ps1, xs1, pxs1))
+
+    def slot(ph, k):
+        return k % 2 if ph == 0 else k - 1
+
     def piece(ph, dr, k, c, excl, xb):
         R = rows_of[ph]
-        q = R // 4
-        row = pl.multiple_of(origin(dr, k) * R + dr * (R // 2) + c * q, q)
+        if ph == 0:
+            q = R // 4
+            row = origin(dr, k) * R + dr * (R // 2) + c * q
+        else:
+            q = R // 2
+            row = origin(dr, k) * R + c * q
+        row = pl.multiple_of(row, q)
         if excl:
             col = pl.multiple_of(xb * (E[ph] + M[ph]), 128)
             return bufs[ph].at[pl.ds(row, q), pl.ds(col, E[ph])]
@@ -64,20 +75,20 @@
         return {"seq": s if seq is None else seq, "dp": d if dp is None else dp}
 
     def ring_desc(ph, dr, k, at, p):
-        return mk(piece(ph, dr, at, core, p == 0, x), rs.at[ph, dr, p, k % 2],
-                  rr.at[ph, dr, k - 1, p], dev(dp=ring_to[dr]))
+        return mk(piece(ph, dr, at, core, p == 0, x), sems[ph][4].at[dr, p, slot(ph, k)],
+                  sems[ph][0].at[dr, p, k - 1], dev(dp=ring_to[dr]))
 
     def part_desc(ph, dr, k, c, p):
-        return mk(piece(ph, dr, k, c, p == 0, x), ps.at[ph, dr, p, k % 2],
-                  pr.at[ph, dr, k - 1, p], dev(seq=partner))
+        return mk(piece(ph, dr, k, c, p == 0, x), sems[ph][5].at[dr, p, slot(ph, k)],
+                  sems[ph][1].at[dr, p, k - 1], dev(seq=partner))
 
     def x_desc(ph, dr, k, xb):
-        return mk(piece(ph, dr, k, core, True, xb), xs.at[ph, dr, k % 2],
-                  xr.at[ph, dr, k - 1], dev(seq=xpeer))
+        return mk(piece(ph, dr, k, core, True, xb), sems[ph][6].at[dr, slot(ph, k)],
+                  sems[ph][2].at[dr, k - 1], dev(seq=xpeer))
 
     def px_desc(ph, dr, k, c):
-        return mk(piece(ph, dr, k, c, True, 1 - x), pxs.at[ph, dr, k % 2],
-                  pxr.at[ph, dr, k - 1], dev(seq=partner))
+        return mk(piece(ph, dr, k, c, True, 1 - x), sems[ph][7].at[dr, slot(ph, k)],
+                  sems[ph][3].at[dr, k - 1], dev(seq=partner))
 
     def send(desc, k):
         @pl.when(k > 2)
@@ -116,6 +127,43 @@
                     part_desc(ph, dr, k, core, p).wait_send()
                 x_desc(ph, dr, k, x).wait_send()
                 px_desc(ph, dr, k, core).wait_send()
+
+    K = N // 2
+
+    def has(dr, k, p):
+        return k < K or (k == K and p == dr)
+
+    every = [(k, dr, p) for k in range(1, K + 1) for dr in (0, 1) for p in (0, 1) if has(dr, k, p)]
+
+    def op(k):
+        for p in (0, 1):
+            for dr in (0, 1):
+                if not has(dr, k, p):
+                    continue
+                ring_desc(1, dr, k, k, p).wait_recv()
+                if has(dr, k + 1, p):
+                    ring_desc(1, dr, k + 1, k, p).start()
+                if p == 0:
+                    x_desc(1, dr, k, x).start()
+                part_desc(1, dr, k, core, p).start()
+        for dr in (0, 1):
+            if has(dr, k - 1, 0) and k > 1:
+                x_desc(1, dr, k - 1, 1 - x).wait_recv()
+                px_desc(1, dr, k - 1, core).start()
+
+    def collect1():
+        for k, dr, p in every:
+            part_desc(1, dr, k, 1 - core, p).wait_recv()
+            if p == 0:
+                px_desc(1, dr, k, 1 - core).wait_recv()
+
+    def drain1():
+        for k, dr, p in every:
+            ring_desc(1, dr, k, k, p).wait_send()
+            part_desc(1, dr, k, core, p).wait_send()
+            if p == 0:
+                x_desc(1, dr, k, x).wait_send()
+                px_desc(1, dr, k, core).wait_send()
 
     R = D // N
     RO = F // N
@@ -133,6 +181,8 @@
         wout, WO.at[pl.ds(pl.multiple_of(d * RO, RO), RO), :], loc_sem.at[6]))
     for c in loads:
         c.start()
+    tok_load = pltpu.make_async_copy(tok_hbm, tok, tok_sem)
+    tok_load.start()
 
     barrier = pltpu.get_barrier_semaphore()
     for who in (dev(dp=ring_to[0]), dev(dp=ring_to[1]), dev(seq=partner), dev(seq=xpeer)):
@@ -181,21 +231,14 @@
             w = jnp.concatenate([W[rows[0], cols], W[rows[1], cols]], axis=0)
             acc[:, cols] += jnp.dot(lhs[...], w, preferred_element_type=F32)
 
+    tok_load.wait()
+
     @pl.loop(0, tiles)
     def _(j):
         cols = pl.ds(pl.multiple_of(j * tile, tile), tile)
         acc[:, cols] = jnp.dot(tok[:, pl.ds(base, R)], W[pl.ds(base, R), cols],
                                preferred_element_type=F32)
 
-    def op(k):
-        @pl.when(k <= N - 1)
-        def _():
-            relay(1, k)
-
-        @pl.when(jnp.logical_and(k >= 2, k <= N))
-        def _():
-            xrelay(1, k - 1)
-
     @pl.loop(1, N + 2)
     def _(t):
         @pl.when(t <= N - 1)
@@ -212,9 +255,10 @@
         def _():
             xrelay(0, t - 1)
 
-        @pl.when(t >= N)
-        def _():
-            op(t - N + 1)
+        for i in (1, 2):
+            @pl.when(t == N + i - 1)
+            def _():
+                op(i)
 
         @pl.when(t >= 3)
         def _():
@@ -250,13 +294,17 @@
         st_send[...] = st_local[...].astype(BF16)
         chain_desc(s + 1).start()
 
+    later = list(range(3, K + 1))
     blk = T // 2
     tri = (lax.broadcasted_iota(jnp.int32, (blk, blk), 1)
            <= lax.broadcasted_iota(jnp.int32, (blk, blk), 0))
 
     @pl.loop(0, H)
     def _(h):
-        op(h + 3)
+        for i, k in enumerate(later):
+            @pl.when(h == (i * H * 3) // (4 * len(later)))
+            def _():
+                op(k)
         for b in (0, 1):
             r = slice(b * blk, (b + 1) * blk)
             q = q_s[h, r, :]
@@ -285,11 +333,6 @@
                     st_send[j] = (keep * st_recv[j].astype(F32) + st_local[j]).astype(BF16)
                 chain_desc(s + 1).start()
 
-    if N > H + 2:
-        @pl.loop(H + 3, N + 1)
-        def _(k):
-            op(k)
-
     ss[...] = jnp.zeros_like(ss)
 
     @pl.loop(0, H)
@@ -299,6 +342,7 @@
         att[h] = a
         ss[...] += a * a
 
+    op(K + 1)
     inv = lax.rsqrt(jnp.sum(ss[...], axis=1, keepdims=True) * (1.0 / F) + 1e-06)
     ss[...] = jnp.broadcast_to(inv, ss.shape)
 
@@ -309,17 +353,19 @@
         gate = 1.0 / (1.0 + jnp.exp(-acc[:, cols_at(gc)]))
         gated[:, cols_at(f)] = (att[h] * ss[...] * gain[:, cols_at(f)] * gate).astype(BF16)
 
-    @pl.loop(1, N)
-    def _(k):
-        collect(1, k)
+    collect1()
 
     @pl.loop(0, D // tile)
     def _(j):
         cols = pl.ds(pl.multiple_of(j * tile, tile), tile)
-        out[:, cols] = jnp.dot(gated[...], WO[:, cols], preferred_element_type=F32).astype(BF16)
+        ob[:, cols] = jnp.dot(gated[...], WO[:, cols], preferred_element_type=F32).astype(BF16)
+        pltpu.make_async_copy(ob.at[:, cols], out.at[:, cols], out_sem.at[j]).start()
 
     drain(0)
-    drain(1)
+    drain1()
+    for j in range(D // tile):
+        cols = pl.ds(j * tile, tile)
+        pltpu.make_async_copy(ob.at[:, cols], out.at[:, cols], out_sem.at[j]).wait()
 
     @pl.when(s < n_seq - 1)
     def _():
@@ -337,12 +383,14 @@
     hbm = pl.BlockSpec(memory_space=pl.ANY)
     dma = pltpu.SemaphoreType.DMA
     n = n_dp - 1
+    m = n_dp // 2
     y = pl.pallas_call(
         functools.partial(fused, n_dp, n_seq),
         out_shape=jax.ShapeDtypeStruct((T, D), BF16),
-        in_specs=[vm, vm, vm, hbm, hbm, hbm],
-        out_specs=vm,
+        in_specs=[hbm, vm, vm, hbm, hbm, hbm],
+        out_specs=hbm,
         scratch_shapes=[
+            pltpu.VMEM((T, D), BF16), pltpu.VMEM((T, D), BF16),
             pltpu.VMEM((D, 4 * F), BF16), pltpu.VMEM((F, D), BF16),
             pltpu.VMEM((T, 4 * F), F32), pltpu.VMEM((T, R), BF16),
             pltpu.VMEM((H, T, hd), BF16), pltpu.VMEM((H, T, hd), BF16),
@@ -352,8 +400,11 @@
             pltpu.VMEM((H, hd, hd), F32), pltpu.VMEM((H, hd, hd), BF16),
             pltpu.VMEM((H, hd, hd), BF16),
             dma((7,)),
-            dma((2, 2, n, 2)), dma((2, 2, n, 2)), dma((2, 2, n)), dma((2, 2, n)),
-            dma((2, 2, 2, 2)), dma((2, 2, 2, 2)), dma((2, 2, 2)), dma((2, 2, 2)),
+            dma, dma((2 * D // F,)),
+            dma((2, 2, n)), dma((2, 2, n)), dma((2, n)), dma((2, n)),
+            dma((2, 2, 2)), dma((2, 2, 2)), dma((2, 2)), dma((2, 2)),
+            dma((2, 2, m)), dma((2, 2, m)), dma((2, m)), dma((2, m)),
+            dma((2, 2, m)), dma((2, 2, m)), dma((2, m)), dma((2, m)),
             dma, dma,
         ],
         compiler_params=pltpu.CompilerParams(

time: 107 us -> 97.8 us (0.914); the launches traced: 106 us -> 95.9 us
  Pallas kernels: 103 us -> 92.7 us
    pallas_call x1, Pallas kernels: 103 us -> 92.7 us  [body(): pl.pallas_call(functools.partial(fused, n_dp, n_seq), out_shape=jax.Shape...]
where the time goes in v2:
time: 97.8 us; the launch traced here: 95.9 us
  Pallas kernels  92.7 us (95%)
  local copies, waits for them, and re-layouts  3.16 us (3%)
    pallas_call x1, Pallas kernels, body(): pl.pallas_call(functools.partial(fused, n_dp, n_seq), out_shape=jax.Shape...  92.7 us
    unnamed x1, local copies, waits for them, and re-layouts  3.16 us

profile of v2, /device:TPU:0, one launch (start us, length us, event | category | flops | bytes accessed | tf_op | source)
XLA Modules:
  0.0 95.9 jit_solution(492875530932720699)
XLA Ops:
  0.0 92.7 %shard_map.64 = bf16[512,2048]{1,0:T(8,128)(2,1)} custom-call(bf16[512,2048]{1,0:T(8,128)(2,1)} %bitcast.5, f32[8,512]{1,0:T(8,128)} %bitcast.6, f32[1,1024]{1,0:T(1,128)} %bitcast.7, bf16[256,3072]{1,0:T(8,128)(2,1)} %wqkv.1, bf16[256,1024]{1,0:T(8,128)(2,1)} %wgate.1, bf16[128,2048]{1,0:T(8,128)(2,1)} %wout.1), custom_call_target="tpu_custom_call" | custom-call | tf_op jit(solution)/shard_map/pallas_call | solution.py:387
  92.7 3.2 %copy.8 = bf16[1,512,2048]{2,1,0:T(8,128)(2,1)} copy(bf16[1,512,2048]{2,1,0:T(8,128)(2,1)} %bitcast.4) | data formatting | bytes 4194304

commit v3 on v1

v3 whole, which is shorter than its diff:
```python
import functools

import jax
import jax.numpy as jnp
from jax import lax
from jax.experimental import pallas as pl
from jax.experimental.pallas import tpu as pltpu
from jax.sharding import PartitionSpec as P

MESH = pl.DeviceIdType.MESH
F32 = jnp.float32
BF16 = jnp.bfloat16


def fused(n_dp, n_seq, tok_hbm, ld, gain, wqkv, wgate, wout, out, tok, ob, W0, W1, WO, acc0, acc1,
          q_s, k_s, v_s, att, ccol, crow, ss, gated, st_local, st_recv, st_send, loc_sem,
          tok_sem, out_sem, rr, pr, xr, pxr, rs, ps, xs, pxs, ch_s, ch_r):
    T, D = tok_hbm.shape
    H = ld.shape[0]
    F = gain.shape[1]
    hd = F // H
    N = n_dp
    s = lax.axis_index("seq")
    d = lax.axis_index("dp")
    core = s % 2
    x = (s // 2) % 2
    partner = s + 1 - 2 * core
    xpeer = s + 2 - 4 * x
    half = N // 2

    def pos_of(i):
        return jnp.where(i % 2 == 0, i // 2, N - 1 - i // 2)

    def dev_at(p):
        p = lax.rem(p + 2 * N, N)
        return jnp.where(p < half, 2 * p, 2 * (N - 1 - p) + 1)

    pos = pos_of(d)
    ring_to = (dev_at(pos + 1), dev_at(pos - 1))

    def origin(dr, k):
        return dev_at(pos - k) if dr == 0 else dev_at(pos + k)

    cols_all = 2 * F
    E = 5 * cols_all // 16
    M = cols_all - 2 * E
    bufs = (W0, W1, WO)
    rows_of = (D // N, D // N, F // N)

    def piece(ph, dr, k, c, excl, xb):
        q = rows_of[ph] // 2
        row = pl.multiple_of(origin(dr, k) * rows_of[ph] + c * q, q)
        if excl:
            col = pl.multiple_of(xb * (E + M), 128)
            return bufs[ph].at[pl.ds(row, q), pl.ds(col, E)]
        return bufs[ph].at[pl.ds(row, q), pl.ds(E, M)]

    def mk(ref, ssem, rsem, dev):
        return pltpu.make_async_remote_copy(
            src_ref=ref, dst_ref=ref, send_sem=ssem, recv_sem=rsem,
            device_id=dev, device_id_type=MESH)

    def dev(seq=None, dp=None):
        return {"seq": s if seq is None else seq, "dp": d if dp is None else dp}

    def ring_desc(ph, dr, k, at, p):
        return mk(piece(ph, dr, at, core, p == 0, x), rs.at[ph, dr, p, k - 1],
                  rr.at[ph, dr, p, k - 1], dev(dp=ring_to[dr]))

    def part_desc(ph, dr, k, c, p):
        return mk(piece(ph, dr, k, c, p == 0, x), ps.at[ph, dr, p, k - 1],
                  pr.at[ph, dr, p, k - 1], dev(seq=partner))

    def x_desc(ph, dr, k, xb):
        return mk(piece(ph, dr, k, core, True, xb), xs.at[ph, dr, k - 1],
                  xr.at[ph, dr, k - 1], dev(seq=xpeer))

    def px_desc(ph, dr, k, c):
        return mk(piece(ph, dr, k, c, True, 1 - x), pxs.at[ph, dr, k - 1],
                  pxr.at[ph, dr, k - 1], dev(seq=partner))

    K = N // 2

    def has(dr, k, p):
        return k < K or (k == K and p == dr)

    def begin(ph):
        for p in (0, 1):
            for dr in (0, 1):
                if has(dr, 1, p):
                    ring_desc(ph, dr, 1, 0, p).start()

    def relay(ph, k, p):
        for dr in (0, 1):
            if not has(dr, k, p):
                continue
            ring_desc(ph, dr, k, k, p).wait_recv()
            if has(dr, k + 1, p):
                ring_desc(ph, dr, k + 1, k, p).start()
            if p == 0:
                x_desc(ph, dr, k, x).start()
            part_desc(ph, dr, k, core, p).start()

    def xrelay(ph, k):
        for dr in (0, 1):
            if has(dr, k, 0):
                x_desc(ph, dr, k, 1 - x).wait_recv()
                px_desc(ph, dr, k, core).start()

    def collect(ph, k):
        for dr in (0, 1):
            for p in (0, 1):
                if has(dr, k, p):
                    part_desc(ph, dr, k, 1 - core, p).wait_recv()
            if has(dr, k, 0):
                px_desc(ph, dr, k, 1 - core).wait_recv()

    def drain(ph):
        for k in range(1, K + 1):
            for dr in (0, 1):
                for p in (0, 1):
                    if has(dr, k, p):
                        ring_desc(ph, dr, k, k, p).wait_send()
                        part_desc(ph, dr, k, core, p).wait_send()
                if has(dr, k, 0):
                    x_desc(ph, dr, k, x).wait_send()
                    px_desc(ph, dr, k, core).wait_send()

    R = D // N
    RO = F // N
    hw = F // 2
    HG = H // 2
    base = pl.multiple_of(d * R, R)
    g1 = hw // 4
    kq, kk0, kv0 = 0, E, E + M
    gcol = (hw, E + hw, E + hw + g1, E + M + hw)
    src_dst = []
    for gi, buf in ((0, W0), (1, W1)):
        o = gi * hw
        src_dst += [
            (wqkv.at[:, pl.ds(o, hw)], buf, 0, hw),
            (wgate.at[:, pl.ds(o, g1)], buf, gcol[0], g1),
            (wqkv.at[:, pl.ds(F + o, hw)], buf, kk0, hw),
            (wgate.at[:, pl.ds(o + g1, 2 * g1)], buf, gcol[1], 2 * g1),
            (wqkv.at[:, pl.ds(2 * F + o, hw)], buf, kv0, hw),
            (wgate.at[:, pl.ds(o + 3 * g1, g1)], buf, gcol[3], g1),
        ]
    loads = [pltpu.make_async_copy(a, buf.at[pl.ds(base, R), pl.ds(c0, w)], loc_sem.at[i])
             for i, (a, buf, c0, w) in enumerate(src_dst)]
    loads.append(pltpu.make_async_copy(
        wout, WO.at[pl.ds(pl.multiple_of(d * RO, RO), RO), :], loc_sem.at[12]))
    for c in loads:
        c.start()
    tok_load = pltpu.make_async_copy(tok_hbm, tok, tok_sem)
    tok_load.start()

    barrier = pltpu.get_barrier_semaphore()
    for who in (dev(dp=ring_to[0]), dev(dp=ring_to[1]), dev(seq=partner), dev(seq=xpeer)):
        pl.semaphore_signal(barrier, inc=1, device_id=who, device_id_type=MESH)

    @pl.when(s > 0)
    def _():
        pl.semaphore_signal(barrier, inc=1, device_id=dev(seq=s - 1), device_id_type=MESH)

    @pl.when(s < n_seq - 1)
    def _():
        pl.semaphore_signal(barrier, inc=1, device_id=dev(seq=s + 1), device_id_type=MESH)
    for c in loads:
        c.wait()
    pl.semaphore_wait(barrier, 4 + jnp.where(s > 0, 1, 0) + jnp.where(s < n_seq - 1, 1, 0))

    begin(0)

    cum = ld[...]
    lane = lax.broadcasted_iota(jnp.int32, (H, T), 1)
    step = 1
    while step < T:
        cum = cum + jnp.where(lane >= step, pltpu.roll(cum, step, 1), 0.0)
        step *= 2
    for h in range(H):
        crow[h] = jnp.broadcast_to(cum[h:h + 1, :], (8, T))
        ccol[h] = jnp.broadcast_to(cum[h:h + 1, :], (hd, T)).T

    tile = hw
    accs = (acc0, acc1)

    def chunk(gi, o, first=False):
        rows = pl.ds(pl.multiple_of(o * R, R), R)

        @pl.loop(0, cols_all // tile)
        def _(j):
            cols = pl.ds(pl.multiple_of(j * tile, tile), tile)
            y = jnp.dot(tok[:, rows], bufs[gi][rows, cols], preferred_element_type=F32)
            if first:
                accs[gi][:, cols] = y
            else:
                accs[gi][:, cols] += y

    tok_load.wait()
    chunk(0, d, True)
    chunk(1, d, True)

    def silu(v):
        return (v / (1.0 + jnp.exp(-v))).astype(BF16)

    def cols_at(c):
        return pl.ds(pl.multiple_of(c, 128), hd)

    def epilogue(gi):
        a = accs[gi]

        @pl.loop(0, HG)
        def _(i):
            h = gi * HG + i
            kk = silu(a[:, cols_at(kk0 + i * hd)])
            vv = silu(a[:, cols_at(kv0 + i * hd)])
            k_s[h] = kk
            v_s[h] = vv
            q_s[h] = silu(a[:, cols_at(i * hd)])
            c = ccol[h]
            sk = (kk.astype(F32) * jnp.exp(c[T - 1:T, :] - c)).astype(BF16)
            st_local[h] = lax.dot_general(sk, vv, (((0,), (0,)), ((), ())),
                                          preferred_element_type=F32)

        @pl.when(s == 0)
        def _():
            for i in range(gi * HG, (gi + 1) * HG):
                st_recv[i] = jnp.zeros((hd, hd), BF16)
                st_send[i] = st_local[i].astype(BF16)
            chain_desc(gi, s + 1).start()

    def chain_desc(gi, to):
        part = pl.ds(gi * HG, HG)
        return pltpu.make_async_remote_copy(
            src_ref=st_send.at[part], dst_ref=st_recv.at[part], send_sem=ch_s.at[gi],
            recv_sem=ch_r.at[gi], device_id=dev(seq=to), device_id_type=MESH)

    blk = T // 2
    tri = (lax.broadcasted_iota(jnp.int32, (blk, blk), 1)
           <= lax.broadcasted_iota(jnp.int32, (blk, blk), 0))

    def attend(h):
        for b in (0, 1):
            r = slice(b * blk, (b + 1) * blk)
            q = q_s[h, r, :]
            c = jnp.concatenate([ccol[h, r, :]] * (blk // hd), axis=1)
            total = None
            for e in range(b + 1):
                z = slice(e * blk, (e + 1) * blk)
                sc = lax.dot_general(q, k_s[h, z, :], (((1,), (1,)), ((), ())),
                                     preferred_element_type=F32)
                gap = c - crow[h, 0:1, z]
                if e == b:
                    gap = jnp.where(tri, gap, -1e30)
                w = (sc * jnp.exp(gap)).astype(BF16)
                y = jnp.dot(w, v_s[h, z, :], preferred_element_type=F32)
                total = y if total is None else total + y
            att[h, r, :] = total

    def attend_range(lo, hi):
        @pl.loop(lo, hi)
        def _(h):
            attend(h)

    def chain(gi, mine):
        @pl.when(jnp.logical_and(s > 0, mine))
        def _():
            chain_desc(gi, s).wait_recv()

            @pl.when(s < n_seq - 1)
            def _():
                for j in range(gi * HG, (gi + 1) * HG):
                    keep = jnp.exp(ccol[j, T - 1:T, :])
                    st_send[j] = (keep * st_recv[j].astype(F32) + st_local[j]).astype(BF16)
                chain_desc(gi, s + 1).start()

    def grow(gi, k, dr):
        if dr == 0:
            collect(gi, k)
        if k < K or dr == 0:
            chunk(gi, origin(dr, k))

    slots = [(ph, k) for ph in (0, 1, 2) for k in range(1, K + 1)]
    mid = HG // 2
    for i, (ph, k) in enumerate(slots):
        relay(ph, k, 0)
        if i >= 2 and slots[i - 2][0] < 2:
            grow(*slots[i - 2], 0)
        if ph == 2 and k == 3:
            epilogue(1)
        if ph == 1 and k == 3:
            epilogue(0)
        if ph == 1 and k == K:
            attend_range(mid, HG)
        if ph == 2 and k == K:
            chain(1, s < n_seq // 2)
            attend_range(HG, HG + mid)
        relay(ph, k, 1)
        if k == K - 1 and ph < 2:
            begin(ph + 1)
        if i >= 1:
            xrelay(*slots[i - 1])
        if i >= 2 and slots[i - 2][0] < 2:
            grow(*slots[i - 2], 1)
        if ph == 1 and k == 3:
            attend_range(0, mid)
        if ph == 1 and k == K:
            chain(0, s < n_seq // 2)
        if ph == 2 and k == 1:
            chain(0, s >= n_seq // 2)
    attend_range(HG + mid, H)
    chain(1, s >= n_seq // 2)
    xrelay(2, K)

    ss[...] = jnp.zeros_like(ss)

    @pl.loop(0, H)
    def _(h):
        inter = jnp.dot(q_s[h], st_recv[h], preferred_element_type=F32)
        a = att[h] + inter * jnp.exp(ccol[h])
        att[h] = a
        ss[...] += a * a

    inv = lax.rsqrt(jnp.sum(ss[...], axis=1, keepdims=True) * (1.0 / F) + 1e-06)
    ss[...] = jnp.broadcast_to(inv, ss.shape)

    for h in range(H):
        i = h % HG
        gate = 1.0 / (1.0 + jnp.exp(-accs[h // HG][:, gcol[i]:gcol[i] + hd]))
        f = slice(h * hd, (h + 1) * hd)
        gated[:, f] = (att[h] * ss[...] * gain[:, f] * gate).astype(BF16)

    for k in range(1, K + 1):
        collect(2, k)

    @pl.loop(0, D // tile)
    def _(j):
        cols = pl.ds(pl.multiple_of(j * tile, tile), tile)
        ob[:, cols] = jnp.dot(gated[...], WO[:, cols], preferred_element_type=F32).astype(BF16)
        pltpu.make_async_copy(ob.at[:, cols], out.at[:, cols], out_sem.at[j]).start()

    for ph in (0, 1, 2):
        drain(ph)
    for j in range(D // tile):
        cols = pl.ds(j * tile, tile)
        pltpu.make_async_copy(ob.at[:, cols], out.at[:, cols], out_sem.at[j]).wait()

    @pl.when(s < n_seq - 1)
    def _():
        chain_desc(0, s + 1).wait_send()
        chain_desc(1, s + 1).wait_send()


def body(n_dp, n_seq, tokens, log_decay, w_qkv, w_gate, w_out, norm_gain):
    tok = tokens[0]
    T, D = tok.shape
    H = log_decay.shape[1]
    F = norm_gain.shape[0]
    hd = F // H
    vm = pl.BlockSpec(memory_space=pltpu.VMEM)
    hbm = pl.BlockSpec(memory_space=pl.ANY)
    dma = pltpu.SemaphoreType.DMA
    m = n_dp // 2
    y = pl.pallas_call(
        functools.partial(fused, n_dp, n_seq),
        out_shape=jax.ShapeDtypeStruct((T, D), BF16),
        in_specs=[hbm, vm, vm, hbm, hbm, hbm],
        out_specs=hbm,
        scratch_shapes=[
            pltpu.VMEM((T, D), BF16), pltpu.VMEM((T, D), BF16),
            pltpu.VMEM((D, 2 * F), BF16), pltpu.VMEM((D, 2 * F), BF16), pltpu.VMEM((F, D), BF16),
            pltpu.VMEM((T, 2 * F), F32), pltpu.VMEM((T, 2 * F), F32),
            pltpu.VMEM((H, T, hd), BF16), pltpu.VMEM((H, T, hd), BF16),
            pltpu.VMEM((H, T, hd), BF16), pltpu.VMEM((H, T, hd), F32),
            pltpu.VMEM((H, T, hd), F32), pltpu.VMEM((H, 8, T), F32),
            pltpu.VMEM((T, hd), F32), pltpu.VMEM((T, F), BF16),
            pltpu.VMEM((H, hd, hd), F32), pltpu.VMEM((H, hd, hd), BF16),
            pltpu.VMEM((H, hd, hd), BF16),
            dma((13,)), dma, dma((2 * D // F,)),
            dma((3, 2, 2, m)), dma((3, 2, 2, m)), dma((3, 2, m)), dma((3, 2, m)),
            dma((3, 2, 2, m)), dma((3, 2, 2, m)), dma((3, 2, m)), dma((3, 2, m)),
            dma((2,)), dma((2,)),
        ],
        compiler_params=pltpu.CompilerParams(
            collective_id=0, has_side_effects=True, vmem_limit_bytes=60 * 1024 * 1024),
    )(tok, log_decay[0], norm_gain[None], w_qkv, w_gate, w_out)
    return y[None]


def solution(mesh):
    placed = (
        P("dp", "seq", None),
        P("dp", None, "seq"),
        P("dp", None),
        P("dp", None),
        P("dp", None),
        P(),
    )
    return jax.shard_map(
        functools.partial(body, mesh.shape["dp"], mesh.shape["seq"]),
        mesh=mesh, in_specs=placed, out_specs=P("dp", "seq", None), check_vma=False
    )
```

time: 107 us -> 94.9 us (0.89)
  Pallas kernels: 103 us -> 91.4 us
    pallas_call x1, Pallas kernels: 103 us -> 91.4 us  [body(): pl.pallas_call(functools.partial(fused, n_dp, n_seq), out_shape=jax.Shape...]
where the time goes in v3:
time: 94.9 us; the launch traced here: 94.6 us
  Pallas kernels  91.4 us (96%)
  local copies, waits for them, and re-layouts  3.16 us (3%)
    pallas_call x1, Pallas kernels, body(): pl.pallas_call(functools.partial(fused, n_dp, n_seq), out_shape=jax.Shape...  91.4 us
    unnamed x1, local copies, waits for them, and re-layouts  3.16 us

profile of v3, /device:TPU:0, one launch (start us, length us, event | category | flops | bytes accessed | tf_op | source)
XLA Modules:
  0.0 94.6 jit_solution(16507684022058100050)
XLA Ops:
  0.0 91.4 %shard_map.64 = bf16[512,2048]{1,0:T(8,128)(2,1)} custom-call(bf16[512,2048]{1,0:T(8,128)(2,1)} %bitcast.5, f32[8,512]{1,0:T(8,128)} %bitcast.6, f32[1,1024]{1,0:T(1,128)} %bitcast.7, bf16[256,3072]{1,0:T(8,128)(2,1)} %wqkv.1, bf16[256,1024]{1,0:T(8,128)(2,1)} %wgate.1, bf16[128,2048]{1,0:T(8,128)(2,1)} %wout.1), custom_call_target="tpu_custom_call" | custom-call | tf_op jit(solution)/shard_map/pallas_call | solution.py:364
  91.4 3.2 %copy.8 = bf16[1,512,2048]{2,1,0:T(8,128)(2,1)} copy(bf16[1,512,2048]{2,1,0:T(8,128)(2,1)} %bitcast.4) | data formatting | bytes 4194304

commit v4 on v3

--- a/solution.py
+++ b/solution.py
@@ -287,14 +287,14 @@
         if i >= 2 and slots[i - 2][0] < 2:
             grow(*slots[i - 2], 0)
         if ph == 2 and k == 3:
-            epilogue(1)
+            attend_range(HG, HG + mid)
         if ph == 1 and k == 3:
             epilogue(0)
         if ph == 1 and k == K:
             attend_range(mid, HG)
         if ph == 2 and k == K:
             chain(1, s < n_seq // 2)
-            attend_range(HG, HG + mid)
+            attend_range(HG + mid, H)
         relay(ph, k, 1)
         if k == K - 1 and ph < 2:
             begin(ph + 1)
@@ -304,11 +304,12 @@
             grow(*slots[i - 2], 1)
         if ph == 1 and k == 3:
             attend_range(0, mid)
+        if ph == 2 and k == 2:
+            epilogue(1)
         if ph == 1 and k == K:
             chain(0, s < n_seq // 2)
         if ph == 2 and k == 1:
             chain(0, s >= n_seq // 2)
-    attend_range(HG + mid, H)
     chain(1, s >= n_seq // 2)
     xrelay(2, K)
 

time: 94.9 us -> 95.4 us (level)
  no operation moved by 1% of the time
where the time goes in v4:
time: 95.4 us; the launch traced here: 94.2 us
  Pallas kernels  91.1 us (95%)
  local copies, waits for them, and re-layouts  3.16 us (3%)
    pallas_call x1, Pallas kernels, body(): pl.pallas_call(functools.partial(fused, n_dp, n_seq), out_shape=jax.Shape...  91.1 us
    unnamed x1, local copies, waits for them, and re-layouts  3.16 us

profile of v4, /device:TPU:0, one launch (start us, length us, event | category | flops | bytes accessed | tf_op | source)
XLA Modules:
  0.0 94.2 jit_solution(2814715047206062662)
XLA Ops:
  0.0 91.1 %shard_map.64 = bf16[512,2048]{1,0:T(8,128)(2,1)} custom-call(bf16[512,2048]{1,0:T(8,128)(2,1)} %bitcast.5, f32[8,512]{1,0:T(8,128)} %bitcast.6, f32[1,1024]{1,0:T(1,128)} %bitcast.7, bf16[256,3072]{1,0:T(8,128)(2,1)} %wqkv.1, bf16[256,1024]{1,0:T(8,128)(2,1)} %wgate.1, bf16[128,2048]{1,0:T(8,128)(2,1)} %wout.1), custom_call_target="tpu_custom_call" | custom-call | tf_op jit(solution)/shard_map/pallas_call | solution.py:365
  91.1 3.2 %copy.8 = bf16[1,512,2048]{2,1,0:T(8,128)(2,1)} copy(bf16[1,512,2048]{2,1,0:T(8,128)(2,1)} %bitcast.4) | data formatting | bytes 4194304
